TPU v7x, 256 devices: a whole 4x4x8 slice. The times are simulated.
256 devices in a mesh: ctx: 32 (over y, z), ret: 2 (over core), tp: 4 (over x).
Axes of the slice: x: 4, y: 4, z: 8, core: 2. Of those that a mesh axis runs over, the one named last changes fastest.
Arguments:
- queries: bfloat16 [32768, 2048], P('ctx', 'tp'), may hold values from -256 to 256
- d_attn: bfloat16 [32768, 2048], P('ctx', 'tp'), may hold values from -6 to 6
- pool: bfloat16 [2, 32768, 896], P('ret', 'ctx'), may hold values from -6 to 6
- w_key: bfloat16 [896, 2048], P(None, 'tp'), may hold values from -0.1875 to 0.1875
- w_value: bfloat16 [896, 2048], P(None, 'tp'), may hold values from -0.1875 to 0.1875
- owners: int32 [512, 2], replicated, may hold values from 0 to 31, as said below
- picks: int32 [512, 2], replicated, may hold values from 0 to 1023
- live_counts: int32 [2, 32], replicated, may hold values from 1 to 8
Outputs:
- attn_out: bfloat16 [32768, 2048], P('ctx', 'tp')
- d_queries: bfloat16 [32768, 2048], P('ctx', 'tp')
- d_w_key: bfloat16 [896, 2048], P(None, 'tp')
- d_w_value: bfloat16 [896, 2048], P(None, 'tp')
Inputs may be any that keep to these rules, and one draw needn't show every extreme that they name: `owners`: in each column, at most 1 of the 16 spans of one ctx slab name the same owner, and in every slab some owner is named exactly 1 times.
All inputs are finite; a program needn't handle non-finite values.
Results may differ from a plain program's by a relative error of at most 0.0095.
The roundings to bfloat16 on the way count: a program that leaves them out, or rounds other values in their place, can miss the bound.
Values may be sent and summed in bfloat16 or wider, within the bound.
No kernel may reach another device: no remote copies, remote signals or barrier semaphores. Data moves between devices by JAX's collectives and lax.ppermute only.
A program may use at most 128 MiB of HBM per device.

v0:
```python
import math
import jax
import jax.numpy as jnp
from jax import lax
from jax.sharding import PartitionSpec as P

HEAD_DIM = 128
SPAN = 64
NBR_LEN = 128
CH_DEV = 16


def combined_all(x, axis, combine):
    everything = jax.tree.map(lambda part: lax.all_gather(part, axis), x)
    leading = jax.tree.map(lambda part: part[0], everything)

    def hop(k, so_far):
        return combine(so_far, jax.tree.map(lambda part: part[k], everything))

    return lax.fori_loop(1, lax.axis_size(axis), hop, leading)


def combine_stats(earlier, later):
    first_max, first_total = earlier
    second_max, second_total = later
    joint_max = jnp.maximum(first_max, second_max)
    joint_total = first_total * jnp.exp(first_max - joint_max) + second_total * jnp.exp(
        second_max - joint_max
    )
    return (joint_max, joint_total)


def body(queries, d_attn, pool, w_key, w_value, owners, picks, live_counts):
    ctx_count = lax.axis_size("ctx")
    ctx_place = lax.axis_index("ctx")
    ret_place = lax.axis_index("ret")
    capacity = (CH_DEV + ctx_count - 1) // ctx_count
    head_cols = w_key.shape[1]
    local_heads = head_cols // HEAD_DIM
    blocks = pool.shape[1] // NBR_LEN
    enc_width = pool.shape[2]
    score_scale = 1.0 / math.sqrt(HEAD_DIM)
    owner_col = lax.dynamic_index_in_dim(owners, ret_place, 1, keepdims=False)
    pick_col = lax.dynamic_index_in_dim(picks, ret_place, 1, keepdims=False)
    count_row = lax.dynamic_index_in_dim(live_counts, ret_place, 0, keepdims=False)
    owner_ids = jnp.arange(ctx_count, dtype=jnp.int32)
    counts_of = jnp.sum(
        jnp.where(owner_col[:, None] == owner_ids[None, :], count_row[None, :], 0), axis=1
    )
    slot_col = pick_col % counts_of
    owner_grid = owner_col.reshape(ctx_count, CH_DEV)
    slot_grid = slot_col.reshape(ctx_count, CH_DEV)
    position = jnp.arange(CH_DEV, dtype=jnp.int32)
    earlier = position[None, :] < position[:, None]
    same_owner = owner_grid[:, :, None] == owner_grid[:, None, :]
    request_rank = jnp.sum(jnp.logical_and(same_owner, earlier[None]), axis=2)
    places = jnp.arange(capacity, dtype=jnp.int32)
    wanted = jnp.logical_and(
        (owner_grid == ctx_place)[:, None, :], request_rank[:, None, :] == places[None, :, None]
    )
    send_slot = jnp.sum(jnp.where(wanted, slot_grid[:, None, :], 0), axis=2).reshape(-1)
    send_live = jnp.any(wanted, axis=2).reshape(-1)
    my_owner = lax.dynamic_index_in_dim(owner_grid, ctx_place, 0, keepdims=False)
    my_rank = lax.dynamic_index_in_dim(request_rank, ctx_place, 0, keepdims=False)
    recv_index = my_owner * capacity + my_rank
    pool_blocks = pool[0].reshape(blocks, NBR_LEN, enc_width)
    flat_pool = pool[0]
    own_keys = jnp.dot(flat_pool, w_key, preferred_element_type=jnp.float32).astype(jnp.bfloat16)
    own_values = jnp.dot(flat_pool, w_value, preferred_element_type=jnp.float32).astype(
        jnp.bfloat16
    )
    own_pair = jnp.concatenate([own_keys, own_values], axis=1).reshape(
        blocks, NBR_LEN, 2 * head_cols
    )
    outgoing = jnp.take(own_pair, send_slot, axis=0)
    incoming = lax.all_to_all(outgoing, "ctx", split_axis=0, concat_axis=0, tiled=True)
    chosen = jnp.take(incoming, recv_index, axis=0)
    key_tiles = chosen[:, :, :head_cols]
    value_tiles = chosen[:, :, head_cols:]
    query_tiles = queries.reshape(CH_DEV, SPAN, local_heads, HEAD_DIM)
    grad_out = d_attn.reshape(CH_DEV, SPAN, local_heads, HEAD_DIM)
    key_four = key_tiles.reshape(CH_DEV, NBR_LEN, local_heads, HEAD_DIM)
    value_four = value_tiles.reshape(CH_DEV, NBR_LEN, local_heads, HEAD_DIM)
    scores = (
        jnp.einsum("cmhd,clhd->chml", query_tiles, key_four, preferred_element_type=jnp.float32)
        * score_scale
    )
    local_max = jnp.max(scores, axis=3)
    local_total = jnp.sum(jnp.exp(scores - local_max[..., None]), axis=3)
    row_max, row_total = combined_all((local_max, local_total), "ret", combine_stats)
    attn_prob = jnp.exp(scores - row_max[..., None]) / row_total[..., None]
    prob_bf = attn_prob.astype(jnp.bfloat16)
    partial_value = jnp.einsum(
        "chml,clhd->cmhd", prob_bf, value_four, preferred_element_type=jnp.float32
    )
    attn_full = lax.psum(partial_value.reshape(CH_DEV * SPAN, head_cols), "ret")
    attn_out = attn_full.astype(jnp.bfloat16)
    out_dot = jnp.sum(
        grad_out.astype(jnp.float32)
        * attn_out.reshape(CH_DEV, SPAN, local_heads, HEAD_DIM).astype(jnp.float32),
        axis=3,
    )
    out_dot = jnp.transpose(out_dot, (0, 2, 1))
    grad_prob = jnp.einsum(
        "cmhd,clhd->chml", grad_out, value_four, preferred_element_type=jnp.float32
    )
    dscore = (attn_prob * (grad_prob - out_dot[..., None]) * score_scale).astype(jnp.bfloat16)
    dq_part = jnp.einsum("chml,clhd->cmhd", dscore, key_four, preferred_element_type=jnp.float32)
    d_queries = lax.psum(dq_part.reshape(CH_DEV * SPAN, head_cols), "ret").astype(jnp.bfloat16)
    key_grad = jnp.einsum(
        "chml,cmhd->clhd", dscore, query_tiles, preferred_element_type=jnp.float32
    ).astype(jnp.bfloat16)
    value_grad = jnp.einsum(
        "chml,cmhd->clhd", prob_bf, grad_out, preferred_element_type=jnp.float32
    ).astype(jnp.bfloat16)
    grad_pair = jnp.concatenate(
        [
            key_grad.reshape(CH_DEV, NBR_LEN, head_cols),
            value_grad.reshape(CH_DEV, NBR_LEN, head_cols),
        ],
        axis=2,
    )
    mean_share = 1.0 / (CH_DEV * ctx_count)
    back_hit = recv_index[None, :] == jnp.arange(ctx_count * capacity, dtype=jnp.int32)[:, None]
    back_span = jnp.sum(jnp.where(back_hit, position[None, :], 0), axis=1)
    returning = jnp.take(grad_pair, back_span, axis=0)
    arrived = lax.all_to_all(returning, "ctx", split_axis=0, concat_axis=0, tiled=True)
    arrived = arrived * send_live[:, None, None].astype(jnp.bfloat16)
    source = jnp.take(pool_blocks, send_slot, axis=0).reshape(-1, enc_width)
    weight_part = (
        jnp.einsum(
            "re,rk->ek",
            source,
            arrived.reshape(-1, 2 * head_cols),
            preferred_element_type=jnp.float32,
        )
        * mean_share
    )
    weight_sum = lax.psum(weight_part, ("ctx", "ret"))
    d_w_key = weight_sum[:, :head_cols].astype(jnp.bfloat16)
    d_w_value = weight_sum[:, head_cols:].astype(jnp.bfloat16)
    return (attn_out, d_queries, d_w_key, d_w_value)


def solution(mesh):
    return jax.shard_map(
        body,
        mesh=mesh,
        in_specs=(
            P("ctx", "tp"),
            P("ctx", "tp"),
            P("ret", "ctx", None),
            P(None, "tp"),
            P(None, "tp"),
            P(),
            P(),
            P(),
        ),
        out_specs=(P("ctx", "tp"), P("ctx", "tp"), P(None, "tp"), P(None, "tp")),
        check_vma=False,
    )
```

profile of v0, /device:TPU:2, one launch (start us, length us, event | category | flops | bytes accessed | tf_op | source)
XLA Modules:
  0.0 822.3 jit_solution(8104515446239602236)
XLA Ops:
  10.8 4.0 copy.102
  14.8 6.5 gather_fusion
  21.3 7.5 broadcast_select_fusion.1
  28.8 11.7 %all-to-all-start = ((bf16[32,128,1024]{2,1,0:T(8,128)(2,1)}), bf16[32,128,1024]{2,1,0:T(8,128)(2,1)}, u32[]{:S(2)}, u32[]{:S(2)}) async-start(bf16[32,128,1024]{2,1,0:T(8,128)(2,1)} %broadcast_select_fusion.1), calls=%async_computation | async-start | bytes 16777216 | tf_op jit(solution)/shard_map/all_to_all | solution.py:76
  43.0 184.8 %all-to-all-done = bf16[32,128,1024]{2,1,0:T(8,128)(2,1)} async-done(((bf16[32,128,1024]{2,1,0:T(8,128)(2,1)}), bf16[32,128,1024]{2,1,0:T(8,128)(2,1)}, u32[]{:S(2)}, u32[]{:S(2)}) %all-to-all-start) | async-done | bytes 8388640 | tf_op jit(solution)/shard_map/all_to_all | solution.py:76
  227.8 6.2 gather_fusion.1
  239.2 4.0 copy.82
  243.1 3.9 copy.81
  254.9 3.1 convolution_convert_fusion
  258.0 3.9 copy.95
  267.8 9.9 %all-reduce.3 = bf16[1024,512]{1,0:T(8,128)(2,1)} all-reduce(f32[1024,512]{1,0:T(8,128)} %bitcast.94), channel_id=1, replica_groups=mesh['ctx'=32,'ret'=2,'tp'=4] {'ret'}, use_global_device_ids=true, to_apply=%region_5.6 | all-reduce | flops 524288 | bytes 3145728 | tf_op jit(solution)/shard_map/psum | solution.py:96
  280.5 3.0 multiply_reduce_fusion
  283.7 4.0 fusion.11
  289.8 3.9 copy.94
  293.8 4.8 pad_maximum_fusion
  298.5 7.1 gather_fusion.3
  305.6 7.5 broadcast_select_fusion
  313.1 13.5 %all-to-all-start.1 = ((bf16[32,128,1024]{2,1,0:T(8,128)(2,1)}), bf16[32,128,1024]{2,1,0:T(8,128)(2,1)}, u32[]{:S(2)}, u32[]{:S(2)}) async-start(bf16[32,128,1024]{2,1,0:T(8,128)(2,1)} %broadcast_select_fusion), calls=%async_computation.1 | async-start | bytes 16777216 | tf_op jit(solution)/shard_map/all_to_all | solution.py:127
  326.6 4.4 gather_fusion.2
  330.9 3.1 convolution_bitcast_fusion
  337.0 9.9 %all-reduce.4 = bf16[1024,512]{1,0:T(8,128)(2,1)} all-reduce(f32[1024,512]{1,0:T(8,128)} %bitcast.97), channel_id=1, replica_groups=mesh['ctx'=32,'ret'=2,'tp'=4] {'ret'}, use_global_device_ids=true, to_apply=%region_7.8 | all-reduce | flops 524288 | bytes 3145728 | tf_op jit(solution)/shard_map/psum | solution.py:109
  346.9 169.6 %all-to-all-done.1 = bf16[32,128,1024]{2,1,0:T(8,128)(2,1)} async-done(((bf16[32,128,1024]{2,1,0:T(8,128)(2,1)}), bf16[32,128,1024]{2,1,0:T(8,128)(2,1)}, u32[]{:S(2)}, u32[]{:S(2)}) %all-to-all-start.1) | async-done | bytes 8388640 | tf_op jit(solution)/shard_map/all_to_all | solution.py:127
  516.5 13.8 %bitcast_multiply_fusion = f32[896,1024]{1,0:T(8,128)} fusion(bf16[32,128,1024]{2,1,0:T(8,128)(2,1)} %all-to-all-done.1, bf16[32]{0:T(256)(128)(2,1)S(1)} %convert_element_type.66, bf16[32,128,896]{2,1,0:T(8,128)(2,1)} %gather_fusion.2, pred[32]{0:T(512)(128)(4,1)S(1)} %get-tuple-element.35), kind=kOutput, calls=%fused_computation.13 | convolution fusion | flops 7524974592 | bytes 19398752 | tf_op jit(solution)/shard_map/re,rk->ek/dot_general | solution.py:131
  530.3 289.2 %all-reduce.5 = bf16[896,1024]{1,0:T(8,128)(2,1)} all-reduce(f32[896,1024]{1,0:T(8,128)} %bitcast_multiply_fusion), channel_id=1, replica_groups=mesh['ctx'=32,'ret'=2,'tp'=4] {'ctx','ret'}, use_global_device_ids=true, to_apply=%region_10.11 | all-reduce | flops 917504 | bytes 5505024 | tf_op jit(solution)/shard_map/psum | solution.py:139
  (63 shorter events, 42.2 us)
Async XLA Ops:
  0.6 4.8 copy-start
  5.4 2.6 copy-start.6
  28.7 11.7 %copy-start.5 = (bf16[1024,512]{1,0:T(8,128)(2,1)S(1)}, bf16[1024,512]{1,0:T(8,128)(2,1)}, u32[]{:S(2)}) copy-start(bf16[1024,512]{1,0:T(8,128)(2,1)} %param.9) | copy-start | bytes 3145732
  28.8 199.1 %all-to-all-start = ((bf16[32,128,1024]{2,1,0:T(8,128)(2,1)}), bf16[32,128,1024]{2,1,0:T(8,128)(2,1)}, u32[]{:S(2)}, u32[]{:S(2)}) async-start(bf16[32,128,1024]{2,1,0:T(8,128)(2,1)} %broadcast_select_fusion.1), calls=%async_computation | async-start | bytes 16777216 | tf_op jit(solution)/shard_map/all_to_all | solution.py:76
  249.4 8.5 %copy-start.1 = (f32[16,4,128,64]{2,3,1,0:T(8,128)}, f32[16,4,128,64]{2,3,1,0:T(8,128)S(1)}, u32[]{:S(2)}) copy-start(f32[16,4,128,64]{2,3,1,0:T(8,128)S(1)} %get-tuple-element.33) | copy-start | bytes 6291460
  249.5 5.4 copy-start.2
  287.7 2.1 copy-start.3
  313.1 203.5 %all-to-all-start.1 = ((bf16[32,128,1024]{2,1,0:T(8,128)(2,1)}), bf16[32,128,1024]{2,1,0:T(8,128)(2,1)}, u32[]{:S(2)}, u32[]{:S(2)}) async-start(bf16[32,128,1024]{2,1,0:T(8,128)(2,1)} %broadcast_select_fusion), calls=%async_computation.1 | async-start | bytes 16777216 | tf_op jit(solution)/shard_map/all_to_all | solution.py:127
  326.6 4.4 copy-start.4
where the time goes:
time: 823 us; the launch traced here: 822 us
  waiting for transfers between devices  354 us (43%)
  blocking collectives  313 us (38%)
  local copies, waits for them, and re-layouts  64.5 us (8%)
  matrix products  35.3 us (4%)
  other arithmetic  28.9 us (4%)
  starting transfers between devices  25.2 us (3%)
    psum x1, blocking collectives, body(): weight_sum = lax.psum(weight_part, ('ctx', 'ret'))  289 us
    all_to_all x1, waiting for transfers between devices, body(): lax.all_to_all(outgoing, 'ctx', split_axis=0, concat_axis=0, tiled=True)  185 us
    all_to_all x1, waiting for transfers between devices, body(): lax.all_to_all(returning, 'ctx', split_axis=0, concat_axis=0, tiled=True)  170 us
  transfers between devices with their start and end apart: 2, of which 2 were waited for; matrix products, arithmetic and copies ran while one was open for 2% of the time, Pallas kernels for 0%

commit v1 on v0

--- a/solution.py
+++ b/solution.py
@@ -136,7 +136,8 @@
         )
         * mean_share
     )
-    weight_sum = lax.psum(weight_part, ("ctx", "ret"))
+    inner = lax.psum(weight_part, "ctx")
+    weight_sum = lax.psum(inner, "ret")
     d_w_key = weight_sum[:, :head_cols].astype(jnp.bfloat16)
     d_w_value = weight_sum[:, head_cols:].astype(jnp.bfloat16)
     return (attn_out, d_queries, d_w_key, d_w_value)

time: 823 us -> 734 us (0.89)
  blocking collectives: 313 us -> 32.8 us
  waiting for transfers between devices: 354 us -> 529 us
  between operations: 0.92 us -> 14.3 us
    psum x1 -> x0, blocking collectives: 289 us -> none  [body(): weight_sum = lax.psum(weight_part, ('ctx', 'ret'))]
    psum x0 -> x1, waiting for transfers between devices: none -> 158 us  [body(): inner = lax.psum(weight_part, 'ctx')]
    all_to_all x1, waiting for transfers between devices: 170 us -> 186 us  [body(): lax.all_to_all(returning, 'ctx', split_axis=0, concat_axis=0, tiled=True)]
    psum x1, blocking collectives: 9.89 us -> 18.9 us  [body(): lax.psum(dq_part.reshape(CH_DEV * SPAN, head_cols), 'ret')]
  transfers between devices with their start and end apart: 2 -> 3, of which waited for: 2 -> 3; matrix products, arithmetic and copies ran while one was open for 2% -> 2% of each run, Pallas kernels for 0% -> 0%
where the time goes in v1:
time: 734 us; the launch traced here: 731 us
  waiting for transfers between devices  529 us (72%)
  local copies, waits for them, and re-layouts  65.6 us (9%)
  matrix products  35.3 us (5%)
  blocking collectives  32.8 us (4%)
  other arithmetic  28.9 us (4%)
  starting transfers between devices  25.3 us (3%)
  between operations  14.3 us (2%)
    all_to_all x1, waiting for transfers between devices, body(): lax.all_to_all(returning, 'ctx', split_axis=0, concat_axis=0, tiled=True)  186 us
    all_to_all x1, waiting for transfers between devices, body(): lax.all_to_all(outgoing, 'ctx', split_axis=0, concat_axis=0, tiled=True)  185 us
    psum x1, waiting for transfers between devices, body(): inner = lax.psum(weight_part, 'ctx')  158 us
    psum x1, blocking collectives, body(): lax.psum(dq_part.reshape(CH_DEV * SPAN, head_cols), 'ret')  18.9 us
  transfers between devices with their start and end apart: 3, of which 3 were waited for; matrix products, arithmetic and copies ran while one was open for 2% of the time, Pallas kernels for 0%

profile of v1, /device:TPU:2, one launch (start us, length us, event | category | flops | bytes accessed | tf_op | source)
XLA Modules:
  0.0 731.3 jit_solution(10146903338169970865)
XLA Ops:
  17.3 4.0 copy.102
  21.3 6.5 gather_fusion
  27.8 7.5 %broadcast_select_fusion.1 = bf16[32,128,1024]{2,1,0:T(8,128)(2,1)} fusion(bf16[32,128,1024]{2,1,0:T(8,128)(2,1)} %gather_fusion, pred[32]{0:T(512)(128)(4,1)S(1)} %get-tuple-element.37), kind=kLoop, calls=%fused_computation.7 | loop fusion | flops 4194304 | bytes 16777248 | tf_op jit(solution)/shard_map/jit(_take)/select_n | solution.py:75
  35.3 11.7 %all-to-all-start = ((bf16[32,128,1024]{2,1,0:T(8,128)(2,1)}), bf16[32,128,1024]{2,1,0:T(8,128)(2,1)}, u32[]{:S(2)}, u32[]{:S(2)}) async-start(bf16[32,128,1024]{2,1,0:T(8,128)(2,1)} %broadcast_select_fusion.1), calls=%async_computation | async-start | bytes 16777216 | tf_op jit(solution)/shard_map/all_to_all | solution.py:76
  49.5 184.8 %all-to-all-done = bf16[32,128,1024]{2,1,0:T(8,128)(2,1)} async-done(((bf16[32,128,1024]{2,1,0:T(8,128)(2,1)}), bf16[32,128,1024]{2,1,0:T(8,128)(2,1)}, u32[]{:S(2)}, u32[]{:S(2)}) %all-to-all-start) | async-done | bytes 8388640 | tf_op jit(solution)/shard_map/all_to_all | solution.py:76
  234.4 6.2 gather_fusion.1
  245.7 4.0 copy.82
  249.7 3.9 copy.81
  261.4 3.1 convolution_convert_fusion
  264.5 3.9 copy.95
  274.4 9.9 %all-reduce.6 = bf16[1024,512]{1,0:T(8,128)(2,1)} all-reduce(f32[1024,512]{1,0:T(8,128)} %bitcast.94), channel_id=1, replica_groups=mesh['ctx'=32,'ret'=2,'tp'=4] {'ret'}, use_global_device_ids=true, to_apply=%region_5.6 | all-reduce | flops 524288 | bytes 3145728 | tf_op jit(solution)/shard_map/psum | solution.py:96
  287.0 3.0 multiply_reduce_fusion
  290.2 4.0 fusion.11
  296.4 3.9 copy.94
  300.3 4.8 pad_maximum_fusion
  305.0 7.1 gather_fusion.3
  312.1 7.5 %broadcast_select_fusion = bf16[32,128,1024]{2,1,0:T(8,128)(2,1)} fusion(bf16[32,128,1024]{2,1,0:T(8,128)(2,1)} %gather_fusion.3, pred[32]{0:T(512)(128)(4,1)S(1)} %get-tuple-element.36), kind=kLoop, calls=%fused_computation.6 | loop fusion | flops 4194304 | bytes 16777248 | tf_op jit(solution)/shard_map/jit(_take)/select_n | solution.py:126
  319.6 13.3 %all-to-all-start.1 = ((bf16[32,128,1024]{2,1,0:T(8,128)(2,1)}), bf16[32,128,1024]{2,1,0:T(8,128)(2,1)}, u32[]{:S(2)}, u32[]{:S(2)}) async-start(bf16[32,128,1024]{2,1,0:T(8,128)(2,1)} %broadcast_select_fusion), calls=%async_computation.1 | async-start | bytes 16777216 | tf_op jit(solution)/shard_map/all_to_all | solution.py:127
  333.2 4.4 gather_fusion.2
  337.5 186.2 %all-to-all-done.1 = bf16[32,128,1024]{2,1,0:T(8,128)(2,1)} async-done(((bf16[32,128,1024]{2,1,0:T(8,128)(2,1)}), bf16[32,128,1024]{2,1,0:T(8,128)(2,1)}, u32[]{:S(2)}, u32[]{:S(2)}) %all-to-all-start.1) | async-done | bytes 8388640 | tf_op jit(solution)/shard_map/all_to_all | solution.py:127
  523.7 13.8 %bitcast_multiply_fusion = f32[896,1024]{1,0:T(8,128)} fusion(bf16[32,128,1024]{2,1,0:T(8,128)(2,1)} %all-to-all-done.1, bf16[32]{0:T(256)(128)(2,1)S(1)} %convert_element_type.66, bf16[32,128,896]{2,1,0:T(8,128)(2,1)} %gather_fusion.2, pred[32]{0:T(512)(128)(4,1)S(1)} %get-tuple-element.37), kind=kOutput, calls=%fused_computation.13 | convolution fusion | flops 7524974592 | bytes 19398752 | tf_op jit(solution)/shard_map/re,rk->ek/dot_general | solution.py:131
  538.7 3.1 convolution_bitcast_fusion
  544.7 158.1 %all-reduce.5.cloned.1.call-done = f32[896,1024]{1,0:T(8,128)} async-done(((f32[896,1024]{1,0:T(8,128)}), f32[896,1024]{1,0:T(8,128)}) %all-reduce.5.cloned.1.call-update) | async-done | bytes 3670032 | tf_op jit(solution)/shard_map/psum | solution.py:139
  702.8 18.9 %all-reduce.7 = (bf16[1024,512]{1,0:T(8,128)(2,1)}, bf16[896,1024]{1,0:T(8,128)(2,1)}) all-reduce(f32[1024,512]{1,0:T(8,128)} %bitcast.97, f32[896,1024]{1,0:T(8,128)} %all-reduce.5.cloned.1.call-done), channel_id=1, replica_groups=mesh['ctx'=32,'ret'=2,'tp'=4] {'ret'}, use_global_device_ids=true, to_apply=%region_7.8 | all-reduce | flops 1441792 | bytes 8650752 | tf_op jit(solution)/shard_map/psum | solution.py:109
  (65 shorter events, 43.7 us)
Async XLA Ops:
  7.2 4.8 copy-start
  12.0 2.6 copy-start.6
  35.3 11.7 %copy-start.5 = (bf16[1024,512]{1,0:T(8,128)(2,1)S(1)}, bf16[1024,512]{1,0:T(8,128)(2,1)}, u32[]{:S(2)}) copy-start(bf16[1024,512]{1,0:T(8,128)(2,1)} %param.9) | copy-start | bytes 3145732
  35.3 199.1 %all-to-all-start = ((bf16[32,128,1024]{2,1,0:T(8,128)(2,1)}), bf16[32,128,1024]{2,1,0:T(8,128)(2,1)}, u32[]{:S(2)}, u32[]{:S(2)}) async-start(bf16[32,128,1024]{2,1,0:T(8,128)(2,1)} %broadcast_select_fusion.1), calls=%async_computation | async-start | bytes 16777216 | tf_op jit(solution)/shard_map/all_to_all | solution.py:76
  256.0 8.5 %copy-start.1 = (f32[16,4,128,64]{2,3,1,0:T(8,128)}, f32[16,4,128,64]{2,3,1,0:T(8,128)S(1)}, u32[]{:S(2)}) copy-start(f32[16,4,128,64]{2,3,1,0:T(8,128)S(1)} %get-tuple-element.35) | copy-start | bytes 6291460
  256.0 5.4 copy-start.2
  294.2 2.1 copy-start.3
  319.6 204.1 %all-to-all-start.1 = ((bf16[32,128,1024]{2,1,0:T(8,128)(2,1)}), bf16[32,128,1024]{2,1,0:T(8,128)(2,1)}, u32[]{:S(2)}, u32[]{:S(2)}) async-start(bf16[32,128,1024]{2,1,0:T(8,128)(2,1)} %broadcast_select_fusion), calls=%async_computation.1 | async-start | bytes 16777216 | tf_op jit(solution)/shard_map/all_to_all | solution.py:127
  332.9 369.9 %all-reduce.5.cloned.1.call-start = ((), (), s32[]{:S(2)}) async-start(), calls=%async_computation.2 | async-start | bytes 7340032 | tf_op jit(solution)/shard_map/psum | solution.py:139
  537.4 1.2 copy-start.4
Sparse Core Ops, SparseCore 0:
  537.6 165.1 all-reduce.4
